TPU v7x, 32 devices: a whole 2x2x4 slice. The times are simulated.
32 devices in a mesh: seq: 16 (over z, x, core), head: 2 (over y).
Axes of the slice: x: 2, y: 2, z: 4, core: 2. Of those that a mesh axis runs over, the one named last changes fastest.
Arguments:
- fw_keys: bfloat16 [8192, 4096], P('seq', 'head'), may hold values from -6 to 6
- fw_values: bfloat16 [8192, 4096], P('seq', 'head'), may hold values from -6 to 6
- fw_queries: bfloat16 [8192, 4096], P('seq', 'head'), may hold values from -6 to 6
- rates: float32 [8192, 8], P('seq', 'head'), as said below
- w_gate: bfloat16 [8, 512, 512], P('head'), may hold values from -0.25 to 0.25
- w_up: bfloat16 [8, 512, 512], P('head'), may hold values from -0.25 to 0.25
- w_down: bfloat16 [8, 512, 512], P('head'), may hold values from -0.25 to 0.25
- out_gain: float32 [4096], P('head'), may hold values from 0.1 to 1.9
- att_query: bfloat16 [8192, 4096], P(('seq', 'head')), may hold values from -6 to 6
- att_key: bfloat16 [8192, 1024], P(('seq', 'head')), may hold values from -6 to 6
- att_value: bfloat16 [8192, 1024], P(('seq', 'head')), may hold values from -6 to 6
Outputs:
- block_out: bfloat16 [8192, 4096], P(('seq', 'head'))
Inputs may be any that keep to these rules, and one draw needn't show every extreme that they name: Positive rates whose scale rises along the span by a factor of three, times per-token noise of 1 to 4.
All inputs are finite; a program needn't handle non-finite values.
Results may differ from a plain program's by a relative error of at most 0.0098.
Values may be sent and summed in bfloat16 or wider, within the bound.
A program may use at most 128 MiB of HBM per device.

v0:
```python
import jax
import jax.numpy as jnp
from jax import lax
from jax.sharding import PartitionSpec as P

HD = 128
WINDOW = 256


def from_behind(block, axis, distance):
    devices = range(lax.axis_size(axis))
    route = [(i - distance, i) for i in devices if i - distance in devices]
    return lax.ppermute(block, axis, route)


def fast_hidden(inputs, w_gate, w_up):
    gate = jnp.dot(inputs, w_gate.T, preferred_element_type=jnp.float32)
    up = jnp.dot(inputs, w_up.T, preferred_element_type=jnp.float32)
    return (gate, up, (jax.nn.silu(gate) * up).astype(jnp.bfloat16))


def head_grads(keys, values, rate_col, w_gate, w_up, w_down):
    gate, up, hidden = fast_hidden(keys, w_gate, w_up)
    dval = (-rate_col[:, None] * values.astype(jnp.float32)).astype(jnp.bfloat16)
    g_down = jnp.dot(hidden.T, dval, preferred_element_type=jnp.float32)
    dhid = jnp.dot(dval, w_down.T, preferred_element_type=jnp.float32)
    sig = jax.nn.sigmoid(gate)
    d_gate = (dhid * up * sig * (1.0 + gate * (1.0 - sig))).astype(jnp.bfloat16)
    d_up = (dhid * (gate * sig)).astype(jnp.bfloat16)
    g_gate = jnp.dot(d_gate.T, keys, preferred_element_type=jnp.float32)
    g_up = jnp.dot(d_up.T, keys, preferred_element_type=jnp.float32)
    return jnp.stack([g_gate, g_up, g_down])


def renorm(old, grads):
    old = old.astype(jnp.float32)
    fresh = old - grads
    scale = jnp.sqrt(jnp.sum(old * old, axis=-1, keepdims=True)) / jnp.sqrt(
        jnp.sum(fresh * fresh, axis=-1, keepdims=True) + 1e-06
    )
    return (fresh * scale).astype(jnp.bfloat16)


def apply_head(queries, weights, gain):
    gate, up, hidden = fast_hidden(queries, weights[0], weights[1])
    raw = jnp.dot(hidden, weights[2], preferred_element_type=jnp.float32)
    normed = raw * lax.rsqrt(jnp.mean(raw * raw, axis=-1, keepdims=True) + 1e-06) * gain
    return normed.astype(jnp.bfloat16)


def per_device(
    fw_keys,
    fw_values,
    fw_queries,
    rates,
    w_gate,
    w_up,
    w_down,
    out_gain,
    att_query,
    att_key,
    att_value,
):
    local_heads = w_gate.shape[0]
    width = w_gate.shape[2]
    stacked = jnp.stack([w_gate, w_up, w_down], axis=1)
    grad_list = []
    for head in range(local_heads):
        cols = slice(head * width, (head + 1) * width)
        grad_list.append(
            head_grads(
                fw_keys[:, cols],
                fw_values[:, cols],
                rates[:, head],
                w_gate[head],
                w_up[head],
                w_down[head],
            )
        )
    local_grads = jnp.stack(grad_list)
    shares = lax.psum_scatter(local_grads, "seq", scatter_dimension=2, tiled=True)
    count = shares.shape[2]
    first = lax.axis_index("seq") * count
    old_rows = lax.dynamic_slice_in_dim(stacked, first, count, 2)
    weights = lax.all_gather(renorm(old_rows, shares), "seq", axis=2, tiled=True)
    out_list = []
    for head in range(local_heads):
        cols = slice(head * width, (head + 1) * width)
        out_list.append(apply_head(fw_queries[:, cols], weights[head], out_gain[cols]))
    fw_local = jnp.concatenate(out_list, axis=1)
    fw_tok = lax.all_to_all(fw_local, "head", split_axis=0, concat_axis=1, tiled=True)
    rows = att_query.shape[0]
    kv_heads = att_key.shape[1] // HD
    group = att_query.shape[1] // HD // kv_heads
    reach = (WINDOW - 1) // rows + 1
    pair = jnp.stack([att_key, att_value])
    earlier = []
    moving = pair
    for step in range(reach):
        moving = from_behind(moving, ("seq", "head"), 1)
        earlier.insert(0, moving)
    window_kv = jnp.concatenate(earlier + [pair], axis=1)
    keys = window_kv[0].reshape(-1, kv_heads, HD)
    values = window_kv[1].reshape(-1, kv_heads, HD)
    base = (lax.axis_index("seq") * lax.axis_size("head") + lax.axis_index("head")) * rows
    qpos = base + jnp.arange(rows, dtype=jnp.int32)
    kpos = base - reach * rows + jnp.arange((reach + 1) * rows, dtype=jnp.int32)
    valid = (
        (kpos[None, :] >= 0)
        & (kpos[None, :] <= qpos[:, None])
        & (kpos[None, :] > qpos[:, None] - WINDOW)
    )
    query = att_query.reshape(rows, kv_heads, group, HD)
    scores = jnp.einsum(
        "rkgd,skd->kgrs", query, keys, preferred_element_type=jnp.float32
    ) / jnp.sqrt(jnp.float32(HD))
    scores = jnp.where(valid, scores, -1e30)
    peak = jnp.max(scores, axis=-1, keepdims=True)
    expo = jnp.exp(scores - peak)
    probs = (expo / jnp.sum(expo, axis=-1, keepdims=True)).astype(jnp.bfloat16)
    attn = jnp.einsum("kgrs,skd->rkgd", probs, values, preferred_element_type=jnp.float32).reshape(
        rows, -1
    )
    return (attn + fw_tok.astype(jnp.float32)).astype(jnp.bfloat16)


def solution(mesh):
    return jax.shard_map(
        per_device,
        mesh=mesh,
        in_specs=(
            P("seq", "head"),
            P("seq", "head"),
            P("seq", "head"),
            P("seq", "head"),
            P("head", None, None),
            P("head", None, None),
            P("head", None, None),
            P("head"),
            P(("seq", "head"), None),
            P(("seq", "head"), None),
            P(("seq", "head"), None),
        ),
        out_specs=P(("seq", "head"), None),
        check_vma=False,
    )
```

profile of v0, /device:TPU:0, one launch (start us, length us, event | category | flops | bytes accessed | tf_op | source)
XLA Modules:
  0.0 314.7 jit_solution(5433684488446617662)
XLA Ops:
  6.5 1.8 fusion.64
  8.4 1.5 fusion.70
  27.7 5.2 %pad_maximum_fusion = f32[4,3,512,512]{3,2,1,0:T(8,128)} fusion(f32[1,3,512,512]{3,2,1,0:T(8,128)S(1)} %get-tuple-element.33, f32[1,3,512,512]{3,2,1,0:T(8,128)S(1)} %get-tuple-element.32, f32[1,3,512,512]{3,2,1,0:T(8,128)S(1)} %get-tuple-element.31, f32[1,3,512,512]{3,2,1,0:T(8,128)S(1)} %get-tuple-element.30), kind=kLoop, calls=%fused_computation.5 | loop fusion | flops 9437184 | bytes 25165824 | tf_op jit(solution)/shard_map/stack | solution.py:80
  33.0 137.6 %reduce-scatter.2.cloned.1.call-done = f32[4,3,32,512]{3,2,1,0:T(8,128)} async-done(((f32[4,3,512,512]{3,2,1,0:T(8,128)}), f32[4,3,32,512]{3,2,1,0:T(8,128)}) %reduce-scatter.2.cloned.1.call-update) | async-done | bytes 786448 | tf_op jit(solution)/shard_map/reduce_scatter | solution.py:81
  175.8 4.4 %collective-permute-start = (bf16[2,256,1024]{1,2,0:T(8,128)(2,1)}, bf16[2,256,1024]{1,2,0:T(8,128)(2,1)}, u32[]{:S(2)}, u32[]{:S(2)}) collective-permute-start(bf16[2,256,1024]{1,2,0:T(8,128)(2,1)} %pad_maximum_fusion.2), channel_id=1, source_target_pairs={{0,1},{1,2},{2,3},{3,4},{4,5},{5,6},{6,7},{7,8},{8,9},{9,10},{10,1... | collective-permute-start | bytes 3145736 | tf_op jit(solution)/shard_map/ppermute | solution.py:13
  180.2 2.7 reshape.101
  183.1 18.0 %collective-permute-done = bf16[2,256,1024]{1,2,0:T(8,128)(2,1)} collective-permute-done((bf16[2,256,1024]{1,2,0:T(8,128)(2,1)}, bf16[2,256,1024]{1,2,0:T(8,128)(2,1)}, u32[]{:S(2)}, u32[]{:S(2)}) %collective-permute-start) | collective-permute-done | bytes 1048608 | tf_op jit(solution)/shard_map/ppermute | solution.py:13
  204.5 9.5 %fusion.151 = (f32[8,4,256]{2,1,0:T(4,128)S(1)}, f32[8,4,256,512]{2,3,1,0:T(8,128)}) fusion(pred[256,512]{0,1:T(8,128)(4,1)S(1)} %compare_and_fusion, bf16[512,8,128,1]{0,2,3,1:T(8,128)(2,1)S(1)} %bitcast.227, bf16[256,8,4,128]{3,2,1,0:T(4,128)(2,1)S(1)} %copy-done.6), kind=kOutput, calls=%fused_computation.227 | convolution fusion | flops 1090519552 | bytes 20086784 | tf_op jit(solution)/shard_map/sub | solution.py:119
  214.0 24.6 %all-gather.2.cloned.1.call-done = bf16[4,3,512,512]{3,2,1,0:T(8,128)(2,1)} async-done(((bf16[4,3,32,512]{3,2,1,0:T(8,128)(2,1)}), bf16[4,3,512,512]{3,2,1,0:T(8,128)(2,1)}) %all-gather.2.cloned.1.call-update) | async-done | bytes 6291472 | tf_op jit(solution)/shard_map/all_gather | solution.py:85
  238.6 2.6 convolution_bitcast_fusion.7
  241.2 2.5 multiply_reduce_fusion.3
  243.7 2.5 convolution_bitcast_fusion.5
  246.2 3.4 %multiply_reduce_fusion.2 = (f32[512]{0:T(512)S(1)}, f32[512,512]{0,1:T(8,128)}) fusion(bf16[4,3,512,512]{3,2,1,0:T(8,128)(2,1)} %all-gather.2.cloned.1.call-done, f32[512,512]{1,0:T(8,128)} %convolution_bitcast_fusion.5, bf16[512,2048]{1,0:T(8,128)(2,1)S(1)} %copy-done.8), kind=kOutput, calls=%fused_computation.73 | convolution fusion | flops 538967552 | bytes 3672064 | tf_op jit(solution)/shard_map/dot_general | solution.py:46
  249.6 2.5 convolution_bitcast_fusion.3
  252.1 3.5 %multiply_reduce_fusion.1 = (f32[512]{0:T(512)S(1)}, f32[512,512]{0,1:T(8,128)}) fusion(bf16[4,3,512,512]{3,2,1,0:T(8,128)(2,1)} %all-gather.2.cloned.1.call-done, f32[512,512]{1,0:T(8,128)} %convolution_bitcast_fusion.3, bf16[512,2048]{1,0:T(8,128)(2,1)S(1)} %copy-done.8), kind=kOutput, calls=%fused_computation.66 | convolution fusion | flops 538967552 | bytes 3672064 | tf_op jit(solution)/shard_map/dot_general | solution.py:46
  255.6 2.5 convolution_bitcast_fusion.1
  258.1 3.5 %multiply_reduce_fusion = (f32[512]{0:T(512)S(1)}, f32[512,512]{0,1:T(8,128)}) fusion(bf16[4,3,512,512]{3,2,1,0:T(8,128)(2,1)} %all-gather.2.cloned.1.call-done, f32[512,512]{1,0:T(8,128)} %convolution_bitcast_fusion.1, bf16[512,2048]{1,0:T(8,128)(2,1)S(1)} %copy-done.8), kind=kOutput, calls=%fused_computation.59 | convolution fusion | flops 538967552 | bytes 3672064 | tf_op jit(solution)/shard_map/dot_general | solution.py:46
  265.2 4.1 %all-to-all-start = ((bf16[2,256,2048]{1,2,0:T(8,128)(2,1)}), bf16[2,256,2048]{1,2,0:T(8,128)(2,1)S(1)}, u32[]{:S(2)}, u32[]{:S(2)}) async-start(bf16[2,256,2048]{1,2,0:T(8,128)(2,1)} %bitcast.216), calls=%async_computation.1 | async-start | bytes 4194304 | tf_op jit(solution)/shard_map/all_to_all | solution.py:91
  269.4 9.0 %fusion.4 = f32[8,128,4,256]{3,1,2,0:T(8,128)} fusion(bf16[512,8,128,1]{0,2,3,1:T(8,128)(2,1)S(1)} %bitcast.226, f32[8,4,256,512]{2,3,1,0:T(8,128)} %get-tuple-element.19, f32[8,4,256]{2,1,0:T(4,128)S(1)} %get-tuple-element.18), kind=kOutput, calls=%fused_computation.8 | convolution fusion | flops 1082130432 | bytes 22052864 | tf_op jit(solution)/shard_map/kgrs,skd->rkgd/dot_general | solution.py:121
  278.4 5.6 %copy.46 = f32[256,4096]{1,0:T(8,128)} copy(f32[256,4096]{0,1:T(8,128)} %bitcast.224) | data formatting | bytes 8388608 | tf_op jit(solution)/shard_map/reshape | solution.py:121
  284.0 10.6 %all-to-all-done = bf16[2,256,2048]{1,2,0:T(8,128)(2,1)S(1)} async-done(((bf16[2,256,2048]{1,2,0:T(8,128)(2,1)}), bf16[2,256,2048]{1,2,0:T(8,128)(2,1)S(1)}, u32[]{:S(2)}, u32[]{:S(2)}) %all-to-all-start) | async-done | bytes 2097184 | tf_op jit(solution)/shard_map/all_to_all | solution.py:91
  294.6 2.3 convert_element_type.141
  296.9 5.7 %copy.47 = f32[256,4096]{1,0:T(8,128)} copy(f32[256,4096]{0,1:T(8,128)} %bitcast.215) | data formatting | bytes 8388608 | tf_op jit(solution)/shard_map/convert_element_type | solution.py:124
  302.6 5.3 %add_convert_fusion = bf16[256,4096]{1,0:T(8,128)(2,1)} fusion(f32[256,4096]{1,0:T(8,128)} %copy.46, f32[256,4096]{1,0:T(8,128)} %copy.47), kind=kLoop, calls=%fused_computation.14 | loop fusion | flops 2097152 | bytes 10485760 | tf_op jit(solution)/shard_map/convert_element_type | solution.py:124
  (86 shorter events, 30.1 us)
Async XLA Ops:
  6.5 1.9 copy-start
  6.5 164.1 %reduce-scatter.2.cloned.1.call-start = ((), (), s32[]{:S(2)}) async-start(), calls=%async_computation.2 | async-start | bytes 13369344 | tf_op jit(solution)/shard_map/reduce_scatter | solution.py:81
  6.5 3.4 %copy-start.1 = (bf16[4,512,512]{2,1,0:T(8,128)(2,1)S(1)}, bf16[4,512,512]{2,1,0:T(8,128)(2,1)}, u32[]{:S(2)}) copy-start(bf16[4,512,512]{2,1,0:T(8,128)(2,1)} %param.16) | copy-start | bytes 6291460
  10.0 1.0 copy-start.14
  10.0 1.6 copy-start.7
  10.0 2.2 copy-start.16
  16.6 1.6 copy-start.3
  32.9 137.7 %copy-start.2 = (bf16[4,512,512]{2,1,0:T(8,128)(2,1)S(1)}, bf16[4,512,512]{2,1,0:T(8,128)(2,1)}, u32[]{:S(2)}) copy-start(bf16[4,512,512]{2,1,0:T(8,128)(2,1)} %param.16) | copy-start | bytes 6291460
  32.9 205.6 %all-gather.2.cloned.1.call-start = ((), (), s32[]{:S(2)}) async-start(), calls=%async_computation.3 | async-start | bytes 6684672 | tf_op jit(solution)/shard_map/all_gather | solution.py:85
  170.6 1.5 copy-start.4
  172.1 1.0 copy-start.13
  173.2 7.0 %copy-start.5 = (bf16[256,4096]{1,0:T(8,128)(2,1)S(1)}, bf16[256,4096]{1,0:T(8,128)(2,1)}, u32[]{:S(2)}) copy-start(bf16[256,4096]{1,0:T(8,128)(2,1)} %param.19) | copy-start | bytes 6291460
  175.8 25.3 %collective-permute-start = (bf16[2,256,1024]{1,2,0:T(8,128)(2,1)}, bf16[2,256,1024]{1,2,0:T(8,128)(2,1)}, u32[]{:S(2)}, u32[]{:S(2)}) collective-permute-start(bf16[2,256,1024]{1,2,0:T(8,128)(2,1)} %pad_maximum_fusion.2), channel_id=1, source_target_pairs={{0,1},{1,2},{2,3},{3,4},{4,5},{5,6},{6,7},{7,8},{8,9},{9,10},{10,1... | collective-permute-start | bytes 3145736 | tf_op jit(solution)/shard_map/ppermute | solution.py:13
  180.2 2.7 copy-start.15
  202.5 2.0 copy-start.6
  214.0 27.2 %copy-start.8 = (bf16[512,2048]{1,0:T(8,128)(2,1)S(1)}, bf16[512,2048]{1,0:T(8,128)(2,1)}, u32[]{:S(2)}) copy-start(bf16[512,2048]{1,0:T(8,128)(2,1)} %param.13) | copy-start | bytes 6291460
  261.6 1.2 copy-start.9
  261.6 1.5 copy-start.10
  261.6 1.8 copy-start.11
  265.2 4.1 %copy-start.12 = (bf16[1,512,1024]{1,2,0:T(8,128)(2,1)S(1)}, bf16[1,512,1024]{1,2,0:T(8,128)(2,1)}, u32[]{:S(2)}) copy-start(bf16[1,512,1024]{1,2,0:T(8,128)(2,1)} %get-tuple-element.9) | copy-start | bytes 3145732
  265.2 29.4 %all-to-all-start = ((bf16[2,256,2048]{1,2,0:T(8,128)(2,1)}), bf16[2,256,2048]{1,2,0:T(8,128)(2,1)S(1)}, u32[]{:S(2)}, u32[]{:S(2)}) async-start(bf16[2,256,2048]{1,2,0:T(8,128)(2,1)} %bitcast.216), calls=%async_computation.1 | async-start | bytes 4194304 | tf_op jit(solution)/shard_map/all_to_all | solution.py:91
Sparse Core Ops, SparseCore 0:
  33.1 137.5 reduce-scatter.1
  173.2 65.3 all-gather.1
where the time goes:
time: 316 us; the launch traced here: 315 us
  waiting for transfers between devices  191 us (60%)
  matrix products  57.4 us (18%)
  local copies, waits for them, and re-layouts  22.9 us (7%)
  other arithmetic  21.3 us (7%)
  between operations  13.8 us (4%)
  starting transfers between devices  8.53 us (3%)
    reduce_scatter x1, waiting for transfers between devices, per_device(): lax.psum_scatter(local_grads, 'seq', scatter_dimension=2, tiled=True)  138 us
    all_gather x1, waiting for transfers between devices, per_device(): lax.all_gather(renorm(old_rows, shares), 'seq', axis=2, tiled=True)  24.6 us
    ppermute x1, waiting for transfers between devices, from_behind(): return lax.ppermute(block, axis, route)  18 us
    dot_general x8, matrix products, fast_hidden(): gate = jnp.dot(inputs, w_gate.T, preferred_element_type=jnp.float32)  14.3 us
    dot_general x4, matrix products, apply_head(): raw = jnp.dot(hidden, weights[2], preferred_element_type=jnp.float32)  12.9 us
    all_to_all x1, waiting for transfers between devices, per_device(): lax.all_to_all(fw_local, 'head', split_axis=0, concat_axis=1, tiled=True)  10.6 us
    sub x1, matrix products, per_device(): expo = jnp.exp(scores - peak)  9.52 us
    dot_general x1, matrix products, per_device(): jnp.einsum('kgrs,skd->rkgd', probs, values, preferred_element_type=jnp.fl...  8.99 us
  transfers between devices with their start and end apart: 4, of which 4 were waited for; matrix products, arithmetic and copies ran while one was open for 10% of the time, Pallas kernels for 0%

commit v1 on v0

--- a/solution.py
+++ b/solution.py
@@ -1,6 +1,10 @@
+import functools
+
 import jax
 import jax.numpy as jnp
 from jax import lax
+from jax.experimental import pallas as pl
+from jax.experimental.pallas import tpu as pltpu
 from jax.sharding import PartitionSpec as P
 
 HD = 128
@@ -48,7 +52,7 @@
     return normed.astype(jnp.bfloat16)
 
 
-def per_device(
+def plain_device(
     fw_keys,
     fw_values,
     fw_queries,
@@ -124,6 +128,358 @@
     return (attn + fw_tok.astype(jnp.float32)).astype(jnp.bfloat16)
 
 
+F32 = jnp.float32
+BF16 = jnp.bfloat16
+MESH = pl.DeviceIdType.MESH
+NT = (((1,), (1,)), ((), ()))
+TN = (((0,), (0,)), ((), ()))
+NN = (((1,), (0,)), ((), ()))
+
+
+def mm(a, b, dims):
+    return lax.dot_general(a, b, dims, preferred_element_type=F32)
+
+
+def grads_kernel(k_ref, v_ref, rate_ref, wg_ref, wu_ref, wd_ref, out_ref):
+    head = pl.program_id(0)
+    keys = k_ref[...]
+    lane = lax.broadcasted_iota(jnp.int32, rate_ref.shape, 1)
+    rate = jnp.sum(jnp.where(lane == head, rate_ref[...], 0.0), axis=1, keepdims=True)
+    gate = mm(keys, wg_ref[0], NT)
+    up = mm(keys, wu_ref[0], NT)
+    sig = jax.nn.sigmoid(gate)
+    silu = gate * sig
+    hidden = (silu * up).astype(BF16)
+    dval = (-rate * v_ref[...].astype(F32)).astype(BF16)
+    out_ref[2] = mm(hidden, dval, TN).astype(BF16)
+    dhid = mm(dval, wd_ref[0], NT)
+    d_gate = (dhid * up * sig * (1.0 + gate * (1.0 - sig))).astype(BF16)
+    out_ref[0] = mm(d_gate, keys, TN).astype(BF16)
+    d_up = (dhid * silu).astype(BF16)
+    out_ref[1] = mm(d_up, keys, TN).astype(BF16)
+
+
+def local_grads_call(keys, values, rates, w_gate, w_up, w_down):
+    heads, hidden, width = w_gate.shape
+    tokens = keys.shape[0]
+    col = pl.BlockSpec((tokens, width), lambda h: (0, h))
+    mat = pl.BlockSpec((1, hidden, width), lambda h: (h, 0, 0))
+    flops = heads * 12 * tokens * hidden * width
+    return pl.pallas_call(
+        grads_kernel,
+        grid=(heads,),
+        in_specs=[col, col, pl.BlockSpec(rates.shape, lambda h: (0, 0)), mat, mat, mat],
+        out_specs=pl.BlockSpec((3, hidden, width), lambda h: (h, 0, 0)),
+        out_shape=jax.ShapeDtypeStruct((heads * 3, hidden, width), BF16),
+        cost_estimate=pl.CostEstimate(
+            flops=flops, bytes_accessed=20 * 2**20, transcendentals=heads * tokens * hidden
+        ),
+        compiler_params=pltpu.CompilerParams(vmem_limit_bytes=40 * 2**20),
+    )(keys, values, rates, w_gate, w_up, w_down)
+
+
+def block_kernel(
+    levels,
+    g_ref,
+    old_ref,
+    fwq_ref,
+    gain_ref,
+    q_ref,
+    kp_ref,
+    vp_ref,
+    k_ref,
+    v_ref,
+    out_ref,
+    fresh,
+    total,
+    core_in,
+    *rest,
+):
+    seq = lax.axis_index("seq")
+    side = lax.axis_index("head")
+    steps = len(levels)
+    row_in = rest[:steps]
+    (attn, bias, fw_out, fw_in, core_sems, rs_sems, ag_sems, out_sems, fw_sems) = rest[steps:]
+    mats, hidden, width = total.shape
+    rows = q_ref.shape[0]
+    local_heads = fwq_ref.shape[1] // width
+    kv_heads = k_ref.shape[1] // HD
+    group = q_ref.shape[1] // HD // kv_heads
+    core = lax.rem(seq, 2)
+
+    def partner(bit):
+        return seq + bit * (1 - 2 * lax.rem(seq // bit, 2))
+
+    barrier = pltpu.get_barrier_semaphore()
+    for bit in (1,) + levels:
+        pl.semaphore_signal(
+            barrier, inc=1, device_id=(partner(bit), side), device_id_type=MESH
+        )
+    pl.semaphore_signal(barrier, inc=1, device_id=(seq, 1 - side), device_id_type=MESH)
+    pl.semaphore_wait(barrier, steps + 2)
+
+    pending = []
+
+    def send(src, dst, sems, where, target):
+        copy = pltpu.make_async_remote_copy(
+            src_ref=src,
+            dst_ref=dst,
+            send_sem=sems.at[(0,) + where],
+            recv_sem=sems.at[(1,) + where],
+            device_id=target,
+            device_id_type=MESH,
+        )
+        copy.start()
+        pending.append(copy)
+        return copy
+
+    offsets = [0]
+    for i, bit in enumerate(levels):
+        offsets.append(offsets[-1] + lax.rem(seq // bit, 2) * (hidden >> (i + 1)))
+
+    def held(i):
+        size = hidden >> i
+        return pl.ds(pl.multiple_of(offsets[i], size) if i else 0, size)
+
+    def given(i):
+        size = hidden >> (i + 1)
+        bit = lax.rem(seq // levels[i], 2)
+        return pl.ds(pl.multiple_of(offsets[i] + (1 - bit) * size, size), size)
+
+    first = core * mats
+    other = (1 - core) * mats
+    core_copies = [
+        send(g_ref.at[other + m], core_in.at[m], core_sems, (m,), (partner(1), side))
+        for m in range(mats)
+    ]
+    rs = {}
+    ag = {}
+
+    def reduce_send(i, m):
+        rs[i, m] = send(
+            total.at[m, given(i)],
+            row_in[i].at[m],
+            rs_sems,
+            (i, m),
+            (partner(levels[i]), side),
+        )
+
+    def core_sum(m):
+        core_copies[m].wait_recv()
+        total[m] = (g_ref[first + m].astype(F32) + core_in[m].astype(F32)).astype(BF16)
+        reduce_send(0, m)
+
+    def gather_send(i, m):
+        where = fresh.at[first + m, held(i + 1)]
+        ag[i, m] = send(where, where, ag_sems, (i, m), (partner(levels[i]), side))
+
+    def row_sum(i, m):
+        rs[i, m].wait_recv()
+        part = total[m, held(i + 1)].astype(F32) + row_in[i][m].astype(F32)
+        if i + 1 < steps:
+            total[m, held(i + 1)] = part.astype(BF16)
+            reduce_send(i + 1, m)
+        else:
+            old = old_ref[m].astype(F32)
+            new = old - part
+            scale = jnp.sqrt(jnp.sum(old * old, axis=-1, keepdims=True)) / jnp.sqrt(
+                jnp.sum(new * new, axis=-1, keepdims=True) + 1e-06
+            )
+            fresh[first + m, held(steps)] = (new * scale).astype(BF16)
+            gather_send(steps - 1, m)
+
+    def gathered(i, m):
+        ag[i, m].wait_recv()
+        if i > 0:
+            gather_send(i - 1, m)
+        else:
+            where = fresh.at[first + m]
+            ag[-1, m] = send(where, where, out_sems, (m,), (partner(1), side))
+
+    def attend(kv):
+        cols = slice(kv * HD, (kv + 1) * HD)
+        keys = jnp.concatenate([kp_ref[:, cols], k_ref[:, cols]], axis=0)
+        values = jnp.concatenate([vp_ref[:, cols], v_ref[:, cols]], axis=0)
+
+        def one(j, carry):
+            at = pl.ds(pl.multiple_of((kv * group + j) * HD, HD), HD)
+            scores = mm(q_ref[:, at], keys, NT) * (HD**-0.5) + bias[...]
+            expo = jnp.exp(scores - jnp.max(scores, axis=-1, keepdims=True))
+            probs = (expo / jnp.sum(expo, axis=-1, keepdims=True)).astype(BF16)
+            attn[:, at] = mm(probs, values, NN)
+            return carry
+
+        lax.fori_loop(0, group, one, 0)
+
+    def apply_rows(head, start):
+        cols = pl.ds(pl.multiple_of(head * width, width), width)
+        query = fwq_ref[pl.ds(pl.multiple_of(start, rows), rows), cols]
+        gate = mm(query, fresh[head * 3], NT)
+        up = mm(query, fresh[head * 3 + 1], NT)
+        mid = (gate * jax.nn.sigmoid(gate) * up).astype(BF16)
+        raw = mm(mid, fresh[head * 3 + 2], NN)
+        mean = jnp.mean(raw * raw, axis=-1, keepdims=True)
+        return (raw * lax.rsqrt(mean + 1e-06) * gain_ref[:, cols]).astype(BF16)
+
+    fw = {}
+
+    def apply(slot, head):
+        fw_out[slot] = apply_rows(head, (1 - side) * rows)
+        fw[slot] = send(fw_out.at[slot], fw_in.at[slot], fw_sems, (slot,), (seq, 1 - side))
+        mine = apply_rows(head, side * rows)
+        at = pl.ds(pl.multiple_of((side * local_heads + head) * width, width), width)
+        out_ref[:, at] = (attn[:, at] + mine.astype(F32)).astype(BF16)
+
+    def finish(slot, head):
+        fw[slot].wait_recv()
+        at = pl.ds(pl.multiple_of(((1 - side) * local_heads + head) * width, width), width)
+        out_ref[:, at] = (attn[:, at] + fw_in[slot].astype(F32)).astype(BF16)
+
+    base = (seq * 2 + side) * rows
+    qpos = base + lax.broadcasted_iota(jnp.int32, bias.shape, 0)
+    kpos = base - rows + lax.broadcasted_iota(jnp.int32, bias.shape, 1)
+    valid = (kpos >= 0) & (kpos <= qpos) & (kpos > qpos - WINDOW)
+    bias[...] = jnp.where(valid, 0.0, -1e30)
+
+    for m in range(mats):
+        core_sum(m)
+    fillers = list(range(kv_heads))
+    depth = 2 * steps
+    for wave in range(mats + depth - 1):
+        for i in range(steps):
+            if 0 <= wave - i < mats:
+                row_sum(i, wave - i)
+        for j in range(steps - 1):
+            if 0 <= wave - steps - j < mats:
+                gathered(steps - 1 - j, wave - steps - j)
+        take = 2 if len(fillers) > mats - 1 - wave else 1
+        for _ in range(take):
+            if fillers:
+                attend(fillers.pop(0))
+    for kv in fillers:
+        attend(kv)
+    half = local_heads // 2
+    mine, theirs = core * half, (1 - core) * half
+    for lh in range(half):
+        for m in range(3 * lh, 3 * lh + 3):
+            gathered(0, m)
+        apply(lh, mine + lh)
+        if lh > 0:
+            for m in range(3 * lh - 3, 3 * lh):
+                ag[-1, m].wait_recv()
+            apply(half + lh - 1, theirs + lh - 1)
+    for m in range(3 * half - 3, 3 * half):
+        ag[-1, m].wait_recv()
+    apply(2 * half - 1, theirs + half - 1)
+    for lh in range(half):
+        finish(lh, mine + lh)
+        if lh > 0:
+            finish(half + lh - 1, theirs + lh - 1)
+    finish(2 * half - 1, theirs + half - 1)
+    for copy in pending:
+        copy.wait_send()
+
+
+def per_device(
+    fw_keys,
+    fw_values,
+    fw_queries,
+    rates,
+    w_gate,
+    w_up,
+    w_down,
+    out_gain,
+    att_query,
+    att_key,
+    att_value,
+):
+    count = lax.axis_size("seq")
+    local_heads, hidden, width = w_gate.shape
+    rows = att_query.shape[0]
+    fits = (
+        lax.axis_size("head") == 2
+        and count >= 4
+        and count & (count - 1) == 0
+        and local_heads % 2 == 0
+        and hidden * 2 // count >= 16
+        and rows == WINDOW
+    )
+    if not fits:
+        return plain_device(
+            fw_keys,
+            fw_values,
+            fw_queries,
+            rates,
+            w_gate,
+            w_up,
+            w_down,
+            out_gain,
+            att_query,
+            att_key,
+            att_value,
+        )
+    before_k = from_behind(att_key, ("seq", "head"), 1)
+    before_v = from_behind(att_value, ("seq", "head"), 1)
+    grads = local_grads_call(fw_keys, fw_values, rates, w_gate, w_up, w_down)
+    levels = []
+    bit = 2
+    while bit < count:
+        levels.append(bit)
+        bit *= 2
+    levels = tuple(levels)
+    steps = len(levels)
+    seq = lax.axis_index("seq")
+    offset = 0
+    for i, bit in enumerate(levels):
+        offset = offset + lax.rem(seq // bit, 2) * (hidden >> (i + 1))
+    own = hidden >> steps
+    half = local_heads // 2
+    mats = 3 * half
+    old = jnp.stack(
+        [
+            lax.dynamic_slice(w, (lax.rem(seq, 2) * half, offset, 0), (half, own, width))
+            for w in (w_gate, w_up, w_down)
+        ],
+        axis=1,
+    ).reshape(mats, own, width)
+    dma = pltpu.SemaphoreType.DMA
+    vmem = pl.BlockSpec(memory_space=pltpu.VMEM)
+    return pl.pallas_call(
+        functools.partial(block_kernel, levels),
+        out_shape=jax.ShapeDtypeStruct(att_query.shape, BF16),
+        in_specs=[vmem] * 9,
+        out_specs=vmem,
+        scratch_shapes=[
+            pltpu.VMEM((2 * mats, hidden, width), BF16),
+            pltpu.VMEM((mats, hidden, width), BF16),
+            pltpu.VMEM((mats, hidden, width), BF16),
+            *[pltpu.VMEM((mats, hidden >> (i + 1), width), BF16) for i in range(steps)],
+            pltpu.VMEM(att_query.shape, F32),
+            pltpu.VMEM((rows, 2 * rows), F32),
+            pltpu.VMEM((local_heads, rows, width), BF16),
+            pltpu.VMEM((local_heads, rows, width), BF16),
+            dma((2, mats)),
+            dma((2, steps, mats)),
+            dma((2, steps, mats)),
+            dma((2, mats)),
+            dma((2, local_heads)),
+        ],
+        compiler_params=pltpu.CompilerParams(
+            collective_id=0, has_side_effects=True, vmem_limit_bytes=60 * 2**20
+        ),
+    )(
+        grads,
+        old,
+        fw_queries,
+        out_gain.reshape(1, -1),
+        att_query,
+        before_k,
+        before_v,
+        att_key,
+        att_value,
+    )
+
+
 def solution(mesh):
     return jax.shard_map(
         per_device,

time: 316 us -> 142 us (0.45)
  the two profiles are of different devices: /device:TPU:0 before, /device:TPU:2 now
where the time goes in v1:
time: 142 us
  Pallas kernels  121 us (85%)
  local copies, waits for them, and re-layouts  14.8 us (10%)
  starting transfers between devices  5.34 us (4%)
    pallas_call x1, Pallas kernels, per_device(): pl.pallas_call(functools.partial(block_kernel, levels), out_shape=jax.Sha...  110 us
    unnamed x16, local copies, waits for them, and re-layouts  12.9 us
    pallas_call x1, Pallas kernels, local_grads_call(): pl.pallas_call(grads_kernel, grid=(heads,), in_specs=[col, col, pl.BlockS...  10.8 us
    ppermute x2, starting transfers between devices, from_behind(): return lax.ppermute(block, axis, route)  5.34 us
  transfers between devices with their start and end apart: 2, of which 0 were waited for; matrix products, arithmetic and copies ran while one was open for 3% of the time, Pallas kernels for 8%

profile of v1, /device:TPU:2, one launch (start us, length us, event | category | flops | bytes accessed | tf_op | source)
XLA Modules:
  0.0 142.0 jit_solution(422243057480833691)
XLA Ops:
  0.0 3.4 %collective-permute-start = (bf16[256,1024]{1,0:T(8,128)(2,1)}, bf16[256,1024]{1,0:T(8,128)(2,1)S(1)}, u32[]{:S(2)}, u32[]{:S(2)}) collective-permute-start(bf16[256,1024]{1,0:T(8,128)(2,1)} %k_ref.3), channel_id=1, source_target_pairs={{0,1},{1,2},{2,3},{3,4},{4,5},{5,6},{6,7},{7,8},{8,9},{9,10},{10,1... | collective-permute-start | bytes 1572872 | tf_op jit(solution)/shard_map/ppermute | solution.py:17
  3.4 1.9 %collective-permute-start.1 = (bf16[256,1024]{1,0:T(8,128)(2,1)}, bf16[256,1024]{1,0:T(8,128)(2,1)S(1)}, u32[]{:S(2)}, u32[]{:S(2)}) collective-permute-start(bf16[256,1024]{1,0:T(8,128)(2,1)} %v_ref.3), channel_id=1, source_target_pairs={{0,1},{1,2},{2,3},{3,4},{4,5},{5,6},{6,7},{7,8},{8,9},{9,10},{10,1... | collective-permute-start | bytes 1572872 | tf_op jit(solution)/shard_map/ppermute | solution.py:17
  5.4 0.8 copy.12.rate_ref
  6.3 0.9 dynamic-slice_bitcast_fusion.2
  7.2 1.0 dynamic-slice_bitcast_fusion
  8.2 0.8 pad_maximum_fusion
  9.0 1.6 %copy-done = bf16[4,512,512]{2,1,0:T(8,128)(2,1)S(1)} copy-done((bf16[4,512,512]{2,1,0:T(8,128)(2,1)S(1)}, bf16[4,512,512]{2,1,0:T(8,128)(2,1)}, u32[]{:S(2)}) %copy-start) | copy-done | bytes 2097176
  10.6 0.0 copy-start.1
  10.6 1.6 %copy-done.1 = bf16[4,512,512]{2,1,0:T(8,128)(2,1)S(1)} copy-done((bf16[4,512,512]{2,1,0:T(8,128)(2,1)S(1)}, bf16[4,512,512]{2,1,0:T(8,128)(2,1)}, u32[]{:S(2)}) %copy-start.1) | copy-done | bytes 2097176
  12.2 0.0 copy-start.2
  12.2 1.6 %copy-done.2 = bf16[4,512,512]{2,1,0:T(8,128)(2,1)S(1)} copy-done((bf16[4,512,512]{2,1,0:T(8,128)(2,1)S(1)}, bf16[4,512,512]{2,1,0:T(8,128)(2,1)}, u32[]{:S(2)}) %copy-start.2) | copy-done | bytes 2097176
  13.8 0.0 copy-start.3
  13.8 1.6 %copy-done.3 = bf16[512,2048]{1,0:T(8,128)(2,1)S(1)} copy-done((bf16[512,2048]{1,0:T(8,128)(2,1)S(1)}, bf16[512,2048]{1,0:T(8,128)(2,1)}, u32[]{:S(2)}) %copy-start.3) | copy-done | bytes 2097176
  15.4 0.0 copy-start.4
  15.4 1.6 %copy-done.4 = bf16[512,2048]{1,0:T(8,128)(2,1)S(1)} copy-done((bf16[512,2048]{1,0:T(8,128)(2,1)S(1)}, bf16[512,2048]{1,0:T(8,128)(2,1)}, u32[]{:S(2)}) %copy-start.4) | copy-done | bytes 2097176
  17.0 10.8 %shard_map.109.g_ref = bf16[12,512,512]{2,1,0:T(8,128)(2,1)} custom-call(bf16[512,2048]{1,0:T(8,128)(2,1)S(1)} %copy-done.3, bf16[512,2048]{1,0:T(8,128)(2,1)S(1)} %copy-done.4, f32[512,4]{1,0:T(8,128)S(1)} %copy.12.rate_ref, bf16[4,512,512]{2,1,0:T(8,128)(2,1)S(1)} %copy-done, bf16[4,512,512]{2,1,0:T(8,128)(2,1)S(1)} %copy-done.1, ...), custom_call_target="tpu_custom_call" | custom-call | flops 6442450944 | bytes 20971520 | tf_op jit(solution)/shard_map/pallas_call | solution.py:168
  27.8 0.0 collective-permute-done.kp_ref
  27.8 0.0 copy-start.5
  27.8 0.0 collective-permute-done.1.vp_ref
  27.8 0.0 copy-start.6
  27.8 0.8 copy-done.5
  28.6 0.2 copy-done.6
  28.8 110.1 %shard_map.110 = bf16[256,4096]{1,0:T(8,128)(2,1)} custom-call(bf16[12,512,512]{2,1,0:T(8,128)(2,1)} %shard_map.109.g_ref, bf16[6,64,512]{2,1,0:T(8,128)(2,1)} %bitcast.8, bf16[512,2048]{1,0:T(8,128)(2,1)} %fwq_ref.1, f32[1,2048]{1,0:T(1,128)} %bitcast.9, bf16[256,4096]{1,0:T(8,128)(2,1)} %q_ref.1, bf16[256,1024]{1,0:T(8,128)(2,1)} %copy-done.5, ...), custom_call_target="tpu_custom_call" | custom-call | tf_op jit(solution)/shard_map/pallas_call | solution.py:447
  138.9 3.1 %copy.14 = bf16[256,4096]{1,0:T(8,128)(2,1)} copy(bf16[256,4096]{1,0:T(8,128)(2,1)} %shard_map.110) | data formatting | bytes 4194304
  (1 shorter events, 0.0 us)
Async XLA Ops:
  0.0 27.8 %collective-permute-start = (bf16[256,1024]{1,0:T(8,128)(2,1)}, bf16[256,1024]{1,0:T(8,128)(2,1)S(1)}, u32[]{:S(2)}, u32[]{:S(2)}) collective-permute-start(bf16[256,1024]{1,0:T(8,128)(2,1)} %k_ref.3), channel_id=1, source_target_pairs={{0,1},{1,2},{2,3},{3,4},{4,5},{5,6},{6,7},{7,8},{8,9},{9,10},{10,1... | collective-permute-start | bytes 1572872 | tf_op jit(solution)/shard_map/ppermute | solution.py:17
  3.4 24.4 %collective-permute-start.1 = (bf16[256,1024]{1,0:T(8,128)(2,1)}, bf16[256,1024]{1,0:T(8,128)(2,1)S(1)}, u32[]{:S(2)}, u32[]{:S(2)}) collective-permute-start(bf16[256,1024]{1,0:T(8,128)(2,1)} %v_ref.3), channel_id=1, source_target_pairs={{0,1},{1,2},{2,3},{3,4},{4,5},{5,6},{6,7},{7,8},{8,9},{9,10},{10,1... | collective-permute-start | bytes 1572872 | tf_op jit(solution)/shard_map/ppermute | solution.py:17
  9.0 1.6 %copy-start = (bf16[4,512,512]{2,1,0:T(8,128)(2,1)S(1)}, bf16[4,512,512]{2,1,0:T(8,128)(2,1)}, u32[]{:S(2)}) copy-start(bf16[4,512,512]{2,1,0:T(8,128)(2,1)} %wg_ref.1) | copy-start | bytes 6291460
  10.6 1.6 %copy-start.1 = (bf16[4,512,512]{2,1,0:T(8,128)(2,1)S(1)}, bf16[4,512,512]{2,1,0:T(8,128)(2,1)}, u32[]{:S(2)}) copy-start(bf16[4,512,512]{2,1,0:T(8,128)(2,1)} %wu_ref.1) | copy-start | bytes 6291460
  12.2 1.6 %copy-start.2 = (bf16[4,512,512]{2,1,0:T(8,128)(2,1)S(1)}, bf16[4,512,512]{2,1,0:T(8,128)(2,1)}, u32[]{:S(2)}) copy-start(bf16[4,512,512]{2,1,0:T(8,128)(2,1)} %wd_ref.1) | copy-start | bytes 6291460
  13.8 1.6 %copy-start.3 = (bf16[512,2048]{1,0:T(8,128)(2,1)S(1)}, bf16[512,2048]{1,0:T(8,128)(2,1)}, u32[]{:S(2)}) copy-start(bf16[512,2048]{1,0:T(8,128)(2,1)} %k_ref.2) | copy-start | bytes 6291460
  15.4 1.6 %copy-start.4 = (bf16[512,2048]{1,0:T(8,128)(2,1)S(1)}, bf16[512,2048]{1,0:T(8,128)(2,1)}, u32[]{:S(2)}) copy-start(bf16[512,2048]{1,0:T(8,128)(2,1)} %v_ref.2) | copy-start | bytes 6291460
  27.8 0.8 copy-start.5
  27.8 1.0 copy-start.6

commit v2 on v1

--- a/solution.py
+++ b/solution.py
@@ -140,83 +140,118 @@
     return lax.dot_general(a, b, dims, preferred_element_type=F32)
 
 
-def grads_kernel(k_ref, v_ref, rate_ref, wg_ref, wu_ref, wd_ref, out_ref):
-    head = pl.program_id(0)
-    keys = k_ref[...]
-    lane = lax.broadcasted_iota(jnp.int32, rate_ref.shape, 1)
-    rate = jnp.sum(jnp.where(lane == head, rate_ref[...], 0.0), axis=1, keepdims=True)
-    gate = mm(keys, wg_ref[0], NT)
-    up = mm(keys, wu_ref[0], NT)
+def head_grads_tile(keys, values, rate, w_gate, w_up, w_down):
+    gate = mm(keys, w_gate, NT)
+    up = mm(keys, w_up, NT)
     sig = jax.nn.sigmoid(gate)
     silu = gate * sig
     hidden = (silu * up).astype(BF16)
-    dval = (-rate * v_ref[...].astype(F32)).astype(BF16)
-    out_ref[2] = mm(hidden, dval, TN).astype(BF16)
-    dhid = mm(dval, wd_ref[0], NT)
+    dval = (-rate * values.astype(F32)).astype(BF16)
+    dhid = mm(dval, w_down, NT)
+    yield 2, mm(hidden, dval, TN)
     d_gate = (dhid * up * sig * (1.0 + gate * (1.0 - sig))).astype(BF16)
-    out_ref[0] = mm(d_gate, keys, TN).astype(BF16)
+    yield 0, mm(d_gate, keys, TN)
     d_up = (dhid * silu).astype(BF16)
-    out_ref[1] = mm(d_up, keys, TN).astype(BF16)
-
-
-def local_grads_call(keys, values, rates, w_gate, w_up, w_down):
-    heads, hidden, width = w_gate.shape
-    tokens = keys.shape[0]
-    col = pl.BlockSpec((tokens, width), lambda h: (0, h))
-    mat = pl.BlockSpec((1, hidden, width), lambda h: (h, 0, 0))
-    flops = heads * 12 * tokens * hidden * width
-    return pl.pallas_call(
-        grads_kernel,
-        grid=(heads,),
-        in_specs=[col, col, pl.BlockSpec(rates.shape, lambda h: (0, 0)), mat, mat, mat],
-        out_specs=pl.BlockSpec((3, hidden, width), lambda h: (h, 0, 0)),
-        out_shape=jax.ShapeDtypeStruct((heads * 3, hidden, width), BF16),
-        cost_estimate=pl.CostEstimate(
-            flops=flops, bytes_accessed=20 * 2**20, transcendentals=heads * tokens * hidden
-        ),
-        compiler_params=pltpu.CompilerParams(vmem_limit_bytes=40 * 2**20),
-    )(keys, values, rates, w_gate, w_up, w_down)
+    yield 1, mm(d_up, keys, TN)
 
 
 def block_kernel(
     levels,
-    g_ref,
-    old_ref,
+    fk_hbm,
+    fv_hbm,
+    fwq_hbm,
+    wg_hbm,
+    wu_hbm,
+    wd_hbm,
+    q_hbm,
+    k_hbm,
+    v_hbm,
+    rate_ref,
+    gain_ref,
+    out_ref,
+    fk_ref,
+    fv_ref,
     fwq_ref,
-    gain_ref,
     q_ref,
-    kp_ref,
-    vp_ref,
-    k_ref,
-    v_ref,
-    out_ref,
+    kv_ref,
     fresh,
+    outgo,
     total,
     core_in,
     *rest,
 ):
     seq = lax.axis_index("seq")
     side = lax.axis_index("head")
+    count = lax.axis_size("seq")
     steps = len(levels)
     row_in = rest[:steps]
-    (attn, bias, fw_out, fw_in, core_sems, rs_sems, ag_sems, out_sems, fw_sems) = rest[steps:]
+    row_out = rest[steps : 2 * steps]
+    (
+        attn,
+        bias,
+        fw_out,
+        fw_in,
+        core_sems,
+        rs_sems,
+        ag_sems,
+        out_sems,
+        fw_sems,
+        halo_sems,
+        fk_sems,
+        fv_sems,
+        w_sems,
+        att_sems,
+    ) = rest[2 * steps :]
     mats, hidden, width = total.shape
     rows = q_ref.shape[0]
     local_heads = fwq_ref.shape[1] // width
-    kv_heads = k_ref.shape[1] // HD
+    half = local_heads // 2
+    kv_heads = kv_ref.shape[2] // HD
     group = q_ref.shape[1] // HD // kv_heads
     core = lax.rem(seq, 2)
+    mine, theirs = core * half, (1 - core) * half
+    first = core * mats
 
     def partner(bit):
         return seq + bit * (1 - 2 * lax.rem(seq // bit, 2))
 
+    def local(src, dst, sem):
+        copy = pltpu.make_async_copy(src, dst, sem)
+        copy.start()
+        return copy
+
+    order = []
+    for lh in range(half):
+        order += [theirs + lh, mine + lh]
+    loads = []
+    for slot, head in enumerate(order):
+        cols = pl.ds(pl.multiple_of(head * width, width), width)
+        loads.append(
+            [
+                local(fk_hbm.at[:, cols], fk_ref.at[slot], fk_sems.at[slot]),
+                local(wg_hbm.at[head], fresh.at[head * 3], w_sems.at[0, slot]),
+                local(wu_hbm.at[head], fresh.at[head * 3 + 1], w_sems.at[1, slot]),
+                local(fv_hbm.at[:, cols], fv_ref.at[slot], fv_sems.at[slot]),
+                local(wd_hbm.at[head], fresh.at[head * 3 + 2], w_sems.at[2, slot]),
+            ]
+        )
+    att_loads = [
+        local(q_hbm, q_ref, att_sems.at[0]),
+        local(k_hbm, kv_ref.at[0, pl.ds(rows, rows)], att_sems.at[1]),
+        local(v_hbm, kv_ref.at[1, pl.ds(rows, rows)], att_sems.at[2]),
+    ]
+    fwq_load = local(fwq_hbm, fwq_ref, att_sems.at[3])
+
+    next_dev = (lax.rem(seq + side, count), 1 - side)
+    prev_dev = (lax.rem(seq + count - 1 + side, count), 1 - side)
     barrier = pltpu.get_barrier_semaphore()
     for bit in (1,) + levels:
         pl.semaphore_signal(
             barrier, inc=1, device_id=(partner(bit), side), device_id_type=MESH
         )
-    pl.semaphore_signal(barrier, inc=1, device_id=(seq, 1 - side), device_id_type=MESH)
-    pl.semaphore_wait(barrier, steps + 2)
+    for target in ((seq, 1 - side), next_dev, prev_dev):
+        pl.semaphore_signal(barrier, inc=1, device_id=target, device_id_type=MESH)
+    pl.semaphore_wait(barrier, steps + 4)
 
     pending = []
 
@@ -233,6 +268,11 @@
         pending.append(copy)
         return copy
 
+    halo = [
+        send(src, kv_ref.at[i, pl.ds(0, rows)], halo_sems, (i,), next_dev)
+        for i, src in enumerate((k_hbm, v_hbm))
+    ]
+
     offsets = [0]
     for i, bit in enumerate(levels):
         offsets.append(offsets[-1] + lax.rem(seq // bit, 2) * (hidden >> (i + 1)))
@@ -241,33 +281,34 @@
         size = hidden >> i
         return pl.ds(pl.multiple_of(offsets[i], size) if i else 0, size)
 
-    def given(i):
+    def parts(i):
         size = hidden >> (i + 1)
         bit = lax.rem(seq // levels[i], 2)
-        return pl.ds(pl.multiple_of(offsets[i] + (1 - bit) * size, size), size)
-
-    first = core * mats
-    other = (1 - core) * mats
-    core_copies = [
-        send(g_ref.at[other + m], core_in.at[m], core_sems, (m,), (partner(1), side))
-        for m in range(mats)
-    ]
+        found = []
+        for shift in (bit * size, (1 - bit) * size):
+            found.append(
+                (
+                    pl.ds(pl.multiple_of(offsets[i] + shift, size), size),
+                    pl.ds(pl.multiple_of(shift, size), size),
+                )
+            )
+        return found
+
+    core_copies = {}
     rs = {}
     ag = {}
 
-    def reduce_send(i, m):
+    def split_send(i, m, arrived):
+        kept, given = parts(i)
+        row_out[i][m] = (total[m, given[0]] + arrived[m, given[1]].astype(F32)).astype(BF16)
         rs[i, m] = send(
-            total.at[m, given(i)],
-            row_in[i].at[m],
-            rs_sems,
-            (i, m),
-            (partner(levels[i]), side),
-        )
+            row_out[i].at[m], row_in[i].at[m], rs_sems, (i, m), (partner(levels[i]), side)
+        )
+        total[m, kept[0]] = total[m, kept[0]] + arrived[m, kept[1]].astype(F32)
 
     def core_sum(m):
         core_copies[m].wait_recv()
-        total[m] = (g_ref[first + m].astype(F32) + core_in[m].astype(F32)).astype(BF16)
-        reduce_send(0, m)
+        split_send(0, m, core_in)
 
     def gather_send(i, m):
         where = fresh.at[first + m, held(i + 1)]
@@ -275,12 +316,11 @@
 
     def row_sum(i, m):
         rs[i, m].wait_recv()
-        part = total[m, held(i + 1)].astype(F32) + row_in[i][m].astype(F32)
         if i + 1 < steps:
-            total[m, held(i + 1)] = part.astype(BF16)
-            reduce_send(i + 1, m)
+            split_send(i + 1, m, row_in[i])
         else:
-            old = old_ref[m].astype(F32)
+            part = total[m, held(steps)] + row_in[i][m].astype(F32)
+            old = fresh[first + m, held(steps)].astype(F32)
             new = old - part
             scale = jnp.sqrt(jnp.sum(old * old, axis=-1, keepdims=True)) / jnp.sqrt(
                 jnp.sum(new * new, axis=-1, keepdims=True) + 1e-06
@@ -298,8 +338,8 @@
 
     def attend(kv):
         cols = slice(kv * HD, (kv + 1) * HD)
-        keys = jnp.concatenate([kp_ref[:, cols], k_ref[:, cols]], axis=0)
-        values = jnp.concatenate([vp_ref[:, cols], v_ref[:, cols]], axis=0)
+        keys = kv_ref[0, :, cols]
+        values = kv_ref[1, :, cols]
 
         def one(j, carry):
             at = pl.ds(pl.multiple_of((kv * group + j) * HD, HD), HD)
@@ -326,49 +366,80 @@
     def apply(slot, head):
         fw_out[slot] = apply_rows(head, (1 - side) * rows)
         fw[slot] = send(fw_out.at[slot], fw_in.at[slot], fw_sems, (slot,), (seq, 1 - side))
-        mine = apply_rows(head, side * rows)
+        local_part = apply_rows(head, side * rows)
         at = pl.ds(pl.multiple_of((side * local_heads + head) * width, width), width)
-        out_ref[:, at] = (attn[:, at] + mine.astype(F32)).astype(BF16)
+        out_ref[:, at] = (attn[:, at] + local_part.astype(F32)).astype(BF16)
 
     def finish(slot, head):
         fw[slot].wait_recv()
         at = pl.ds(pl.multiple_of(((1 - side) * local_heads + head) * width, width), width)
         out_ref[:, at] = (attn[:, at] + fw_in[slot].astype(F32)).astype(BF16)
+
+    lane = lax.broadcasted_iota(jnp.int32, rate_ref.shape, 1)
+    for slot, head in enumerate(order):
+        for copy in loads[slot]:
+            copy.wait()
+        rate = jnp.sum(jnp.where(lane == head, rate_ref[...], 0.0), axis=1, keepdims=True)
+        lh, own = slot // 2, slot % 2
+        tiles = head_grads_tile(
+            fk_ref[slot],
+            fv_ref[slot],
+            rate,
+            fresh[head * 3],
+            fresh[head * 3 + 1],
+            fresh[head * 3 + 2],
+        )
+        made = []
+        for kind, grad in tiles:
+            m = 3 * lh + kind
+            made.append(m)
+            if own:
+                total[m] = grad
+            else:
+                outgo[m] = grad.astype(BF16)
+        for m in made:
+            if own:
+                core_sum(m)
+            else:
+                core_copies[m] = send(
+                    outgo.at[m], core_in.at[m], core_sems, (m,), (partner(1), side)
+                )
 
     base = (seq * 2 + side) * rows
     qpos = base + lax.broadcasted_iota(jnp.int32, bias.shape, 0)
     kpos = base - rows + lax.broadcasted_iota(jnp.int32, bias.shape, 1)
     valid = (kpos >= 0) & (kpos <= qpos) & (kpos > qpos - WINDOW)
     bias[...] = jnp.where(valid, 0.0, -1e30)
-
-    for m in range(mats):
-        core_sum(m)
+    for copy in att_loads:
+        copy.wait()
+    for copy in halo:
+        copy.wait_recv()
+
+    turn = [3 * lh + kind for lh in range(half) for kind in (2, 0, 1)]
     fillers = list(range(kv_heads))
-    depth = 2 * steps
-    for wave in range(mats + depth - 1):
+    for wave in range(mats + 2 * steps - 1):
         for i in range(steps):
             if 0 <= wave - i < mats:
-                row_sum(i, wave - i)
+                row_sum(i, turn[wave - i])
         for j in range(steps - 1):
             if 0 <= wave - steps - j < mats:
-                gathered(steps - 1 - j, wave - steps - j)
+                gathered(steps - 1 - j, turn[wave - steps - j])
         take = 2 if len(fillers) > mats - 1 - wave else 1
         for _ in range(take):
             if fillers:
                 attend(fillers.pop(0))
     for kv in fillers:
         attend(kv)
-    half = local_heads // 2
-    mine, theirs = core * half, (1 - core) * half
+    fwq_load.wait()
     for lh in range(half):
-        for m in range(3 * lh, 3 * lh + 3):
+        for m in turn[3 * lh : 3 * lh + 3]:
             gathered(0, m)
         apply(lh, mine + lh)
         if lh > 0:
-            for m in range(3 * lh - 3, 3 * lh):
+            for m in turn[3 * lh - 3 : 3 * lh]:
                 ag[-1, m].wait_recv()
             apply(half + lh - 1, theirs + lh - 1)
-    for m in range(3 * half - 3, 3 * half):
+    for m in turn[3 * half - 3 :]:
         ag[-1, m].wait_recv()
     apply(2 * half - 1, theirs + half - 1)
     for lh in range(half):
@@ -418,9 +489,6 @@
             att_key,
             att_value,
         )
-    before_k = from_behind(att_key, ("seq", "head"), 1)
-    before_v = from_behind(att_value, ("seq", "head"), 1)
-    grads = local_grads_call(fw_keys, fw_values, rates, w_gate, w_up, w_down)
     levels = []
     bit = 2
     while bit < count:
@@ -428,32 +496,29 @@
         bit *= 2
     levels = tuple(levels)
     steps = len(levels)
-    seq = lax.axis_index("seq")
-    offset = 0
-    for i, bit in enumerate(levels):
-        offset = offset + lax.rem(seq // bit, 2) * (hidden >> (i + 1))
-    own = hidden >> steps
-    half = local_heads // 2
-    mats = 3 * half
-    old = jnp.stack(
-        [
-            lax.dynamic_slice(w, (lax.rem(seq, 2) * half, offset, 0), (half, own, width))
-            for w in (w_gate, w_up, w_down)
-        ],
-        axis=1,
-    ).reshape(mats, own, width)
+    tokens = fw_keys.shape[0]
+    mats = 3 * local_heads // 2
     dma = pltpu.SemaphoreType.DMA
     vmem = pl.BlockSpec(memory_space=pltpu.VMEM)
+    anywhere = pl.BlockSpec(memory_space=pl.ANY)
+    lesser = [pltpu.VMEM((mats, hidden >> (i + 1), width), BF16) for i in range(steps)]
     return pl.pallas_call(
         functools.partial(block_kernel, levels),
         out_shape=jax.ShapeDtypeStruct(att_query.shape, BF16),
-        in_specs=[vmem] * 9,
+        in_specs=[anywhere] * 9 + [vmem] * 2,
         out_specs=vmem,
         scratch_shapes=[
+            pltpu.VMEM((local_heads, tokens, width), BF16),
+            pltpu.VMEM((local_heads, tokens, width), BF16),
+            pltpu.VMEM(fw_queries.shape, BF16),
+            pltpu.VMEM(att_query.shape, BF16),
+            pltpu.VMEM((2, 2 * rows, att_key.shape[1]), BF16),
             pltpu.VMEM((2 * mats, hidden, width), BF16),
             pltpu.VMEM((mats, hidden, width), BF16),
+            pltpu.VMEM((mats, hidden, width), F32),
             pltpu.VMEM((mats, hidden, width), BF16),
-            *[pltpu.VMEM((mats, hidden >> (i + 1), width), BF16) for i in range(steps)],
+            *lesser,
+            *lesser,
             pltpu.VMEM(att_query.shape, F32),
             pltpu.VMEM((rows, 2 * rows), F32),
             pltpu.VMEM((local_heads, rows, width), BF16),
@@ -463,20 +528,27 @@
             dma((2, steps, mats)),
             dma((2, mats)),
             dma((2, local_heads)),
+            dma((2, 2)),
+            dma((local_heads,)),
+            dma((local_heads,)),
+            dma((3, local_heads)),
+            dma((4,)),
         ],
         compiler_params=pltpu.CompilerParams(
             collective_id=0, has_side_effects=True, vmem_limit_bytes=60 * 2**20
         ),
     )(
-        grads,
-        old,
+        fw_keys,
+        fw_values,
         fw_queries,
-        out_gain.reshape(1, -1),
+        w_gate,
+        w_up,
+        w_down,
         att_query,
-        before_k,
-        before_v,
         att_key,
         att_value,
+        rates,
+        out_gain.reshape(1, -1),
     )
 
 

time: 142 us -> 127 us (0.89)
  the two profiles are of different devices: /device:TPU:2 before, /device:TPU:0 now
where the time goes in v2:
time: 127 us
  Pallas kernels  122 us (96%)
  local copies, waits for them, and re-layouts  4.68 us (4%)
    pallas_call x1, Pallas kernels, per_device(): pl.pallas_call(functools.partial(block_kernel, levels), out_shape=jax.Sha...  122 us
    unnamed x2, local copies, waits for them, and re-layouts  4.68 us

profile of v2, /device:TPU:0, one launch (start us, length us, event | category | flops | bytes accessed | tf_op | source)
XLA Modules:
  0.0 126.7 jit_solution(10171003215678501844)
XLA Ops:
  0.0 1.5 %copy.12.rate_ref = f32[512,4]{1,0:T(8,128)} copy(f32[512,4]{0,1:T(4,128)} %param.14) | data formatting | bytes 16384 | tf_op args[3]
  1.6 122.0 %shard_map.109 = bf16[256,4096]{1,0:T(8,128)(2,1)} custom-call(bf16[512,2048]{1,0:T(8,128)(2,1)} %fk_hbm.1, bf16[512,2048]{1,0:T(8,128)(2,1)} %fv_hbm.1, bf16[512,2048]{1,0:T(8,128)(2,1)} %fwq_hbm.1, bf16[4,512,512]{2,1,0:T(8,128)(2,1)} %wg_hbm.1, bf16[4,512,512]{2,1,0:T(8,128)(2,1)} %wu_hbm.1, bf16[4,512,512]{2,1,0:T(8,128)(2,1)} %wd_hbm.1, ...), custom_call_target="tpu_custom_call" | custom-call | tf_op jit(solution)/shard_map/pallas_call | solution.py:505
  123.6 3.1 %copy.14 = bf16[256,4096]{1,0:T(8,128)(2,1)} copy(bf16[256,4096]{1,0:T(8,128)(2,1)} %shard_map.109) | data formatting | bytes 4194304

commit v3 on v2

--- a/solution.py
+++ b/solution.py
@@ -9,6 +9,7 @@
 
 HD = 128
 WINDOW = 256
+CUT = 2
 
 
 def from_behind(block, axis, distance):
@@ -220,6 +221,12 @@
         copy.start()
         return copy
 
+    def matrix(head, kind):
+        return pl.ds((head * 3 + kind) * CUT, CUT)
+
+    def weight(head, kind):
+        return fresh[matrix(head, kind)].reshape(CUT * hidden, width)
+
     order = []
     for lh in range(half):
         order += [theirs + lh, mine + lh]
@@ -229,10 +236,10 @@
         loads.append(
             [
                 local(fk_hbm.at[:, cols], fk_ref.at[slot], fk_sems.at[slot]),
-                local(wg_hbm.at[head], fresh.at[head * 3], w_sems.at[0, slot]),
-                local(wu_hbm.at[head], fresh.at[head * 3 + 1], w_sems.at[1, slot]),
+                local(wg_hbm.at[head], fresh.at[matrix(head, 0)], w_sems.at[0, slot]),
+                local(wu_hbm.at[head], fresh.at[matrix(head, 1)], w_sems.at[1, slot]),
                 local(fv_hbm.at[:, cols], fv_ref.at[slot], fv_sems.at[slot]),
-                local(wd_hbm.at[head], fresh.at[head * 3 + 2], w_sems.at[2, slot]),
+                local(wd_hbm.at[head], fresh.at[matrix(head, 2)], w_sems.at[2, slot]),
             ]
         )
     att_loads = [
@@ -354,18 +361,20 @@
     def apply_rows(head, start):
         cols = pl.ds(pl.multiple_of(head * width, width), width)
         query = fwq_ref[pl.ds(pl.multiple_of(start, rows), rows), cols]
-        gate = mm(query, fresh[head * 3], NT)
-        up = mm(query, fresh[head * 3 + 1], NT)
+        gate = mm(query, weight(head, 0), NT)
+        up = mm(query, weight(head, 1), NT)
         mid = (gate * jax.nn.sigmoid(gate) * up).astype(BF16)
-        raw = mm(mid, fresh[head * 3 + 2], NN)
+        raw = mm(mid, weight(head, 2), NN)
         mean = jnp.mean(raw * raw, axis=-1, keepdims=True)
         return (raw * lax.rsqrt(mean + 1e-06) * gain_ref[:, cols]).astype(BF16)
 
     fw = {}
 
-    def apply(slot, head):
+    def apply_send(slot, head):
         fw_out[slot] = apply_rows(head, (1 - side) * rows)
         fw[slot] = send(fw_out.at[slot], fw_in.at[slot], fw_sems, (slot,), (seq, 1 - side))
+
+    def apply_own(head):
         local_part = apply_rows(head, side * rows)
         at = pl.ds(pl.multiple_of((side * local_heads + head) * width, width), width)
         out_ref[:, at] = (attn[:, at] + local_part.astype(F32)).astype(BF16)
@@ -385,18 +394,20 @@
             fk_ref[slot],
             fv_ref[slot],
             rate,
-            fresh[head * 3],
-            fresh[head * 3 + 1],
-            fresh[head * 3 + 2],
+            weight(head, 0),
+            weight(head, 1),
+            weight(head, 2),
         )
         made = []
         for kind, grad in tiles:
-            m = 3 * lh + kind
-            made.append(m)
-            if own:
-                total[m] = grad
-            else:
-                outgo[m] = grad.astype(BF16)
+            for cut in range(CUT):
+                m = (3 * lh + kind) * CUT + cut
+                made.append(m)
+                piece = grad[cut * hidden : (cut + 1) * hidden]
+                if own:
+                    total[m] = piece
+                else:
+                    outgo[m] = piece.astype(BF16)
         for m in made:
             if own:
                 core_sum(m)
@@ -415,7 +426,13 @@
     for copy in halo:
         copy.wait_recv()
 
-    turn = [3 * lh + kind for lh in range(half) for kind in (2, 0, 1)]
+    turn = [
+        (3 * lh + kind) * CUT + cut
+        for lh in range(half)
+        for kind in (2, 0, 1)
+        for cut in range(CUT)
+    ]
+    span = 3 * CUT
     fillers = list(range(kv_heads))
     for wave in range(mats + 2 * steps - 1):
         for i in range(steps):
@@ -432,21 +449,21 @@
         attend(kv)
     fwq_load.wait()
     for lh in range(half):
-        for m in turn[3 * lh : 3 * lh + 3]:
+        now = turn[span * lh : span * (lh + 1)]
+        for m in now:
             gathered(0, m)
-        apply(lh, mine + lh)
-        if lh > 0:
-            for m in turn[3 * lh - 3 : 3 * lh]:
-                ag[-1, m].wait_recv()
-            apply(half + lh - 1, theirs + lh - 1)
-    for m in turn[3 * half - 3 :]:
-        ag[-1, m].wait_recv()
-    apply(2 * half - 1, theirs + half - 1)
+        apply_send(2 * lh, mine + lh)
+        if lh + 1 < half:
+            apply_own(mine + lh)
+        for m in now:
+            ag[-1, m].wait_recv()
+        apply_send(2 * lh + 1, theirs + lh)
+        if lh + 1 == half:
+            apply_own(mine + lh)
+        apply_own(theirs + lh)
     for lh in range(half):
-        finish(lh, mine + lh)
-        if lh > 0:
-            finish(half + lh - 1, theirs + lh - 1)
-    finish(2 * half - 1, theirs + half - 1)
+        finish(2 * lh, mine + lh)
+        finish(2 * lh + 1, theirs + lh)
     for copy in pending:
         copy.wait_send()
 
@@ -472,7 +489,7 @@
         and count >= 4
         and count & (count - 1) == 0
         and local_heads % 2 == 0
-        and hidden * 2 // count >= 16
+        and hidden * 2 // (count * CUT) >= 16
         and rows == WINDOW
     )
     if not fits:
@@ -497,11 +514,13 @@
     levels = tuple(levels)
     steps = len(levels)
     tokens = fw_keys.shape[0]
-    mats = 3 * local_heads // 2
+    mats = 3 * local_heads // 2 * CUT
+    part = hidden // CUT
+    pieces = (local_heads, CUT, part, width)
     dma = pltpu.SemaphoreType.DMA
     vmem = pl.BlockSpec(memory_space=pltpu.VMEM)
     anywhere = pl.BlockSpec(memory_space=pl.ANY)
-    lesser = [pltpu.VMEM((mats, hidden >> (i + 1), width), BF16) for i in range(steps)]
+    lesser = [pltpu.VMEM((mats, part >> (i + 1), width), BF16) for i in range(steps)]
     return pl.pallas_call(
         functools.partial(block_kernel, levels),
         out_shape=jax.ShapeDtypeStruct(att_query.shape, BF16),
@@ -513,10 +532,10 @@
             pltpu.VMEM(fw_queries.shape, BF16),
             pltpu.VMEM(att_query.shape, BF16),
             pltpu.VMEM((2, 2 * rows, att_key.shape[1]), BF16),
-            pltpu.VMEM((2 * mats, hidden, width), BF16),
-            pltpu.VMEM((mats, hidden, width), BF16),
-            pltpu.VMEM((mats, hidden, width), F32),
-            pltpu.VMEM((mats, hidden, width), BF16),
+            pltpu.VMEM((2 * mats, part, width), BF16),
+            pltpu.VMEM((mats, part, width), BF16),
+            pltpu.VMEM((mats, part, width), F32),
+            pltpu.VMEM((mats, part, width), BF16),
             *lesser,
             *lesser,
             pltpu.VMEM(att_query.shape, F32),
@@ -541,9 +560,9 @@
         fw_keys,
         fw_values,
         fw_queries,
-        w_gate,
-        w_up,
-        w_down,
+        w_gate.reshape(pieces),
+        w_up.reshape(pieces),
+        w_down.reshape(pieces),
         att_query,
         att_key,
         att_value,

time: 127 us -> 120 us (0.945)
  Pallas kernels: 122 us -> 115 us
    pallas_call x1, Pallas kernels: 122 us -> 115 us  [per_device(): pl.pallas_call(functools.partial(block_kernel, levels), out_shape=jax.Sha...]
where the time goes in v3:
time: 120 us
  Pallas kernels  115 us (96%)
  local copies, waits for them, and re-layouts  4.68 us (4%)
    pallas_call x1, Pallas kernels, per_device(): pl.pallas_call(functools.partial(block_kernel, levels), out_shape=jax.Sha...  115 us
    unnamed x2, local copies, waits for them, and re-layouts  4.68 us

profile of v3, /device:TPU:0, one launch (start us, length us, event | category | flops | bytes accessed | tf_op | source)
XLA Modules:
  0.0 120.0 jit_solution(16666102995683499880)
XLA Ops:
  0.0 1.5 %copy.12.rate_ref = f32[512,4]{1,0:T(8,128)} copy(f32[512,4]{0,1:T(4,128)} %param.14) | data formatting | bytes 16384 | tf_op args[3]
  1.6 115.3 %shard_map.109 = bf16[256,4096]{1,0:T(8,128)(2,1)} custom-call(bf16[512,2048]{1,0:T(8,128)(2,1)} %fk_hbm.1, bf16[512,2048]{1,0:T(8,128)(2,1)} %fv_hbm.1, bf16[512,2048]{1,0:T(8,128)(2,1)} %fwq_hbm.1, bf16[4,2,256,512]{3,2,1,0:T(8,128)(2,1)} %bitcast.4, bf16[4,2,256,512]{3,2,1,0:T(8,128)(2,1)} %bitcast.5, bf16[4,2,256,512]{3,2,1,0:T(8,128)(2,1)} %bitcast.6, ...), custom_call_target="tpu_custom_call" | custom-call | tf_op jit(solution)/shard_map/pallas_call | solution.py:524
  116.8 3.1 %copy.14 = bf16[256,4096]{1,0:T(8,128)(2,1)} copy(bf16[256,4096]{1,0:T(8,128)(2,1)} %shard_map.109) | data formatting | bytes 4194304
